TPU v7x, 32 devices: a whole 2x2x4 slice. The times are simulated.
32 devices in a mesh: pairs: 2 (over x), rows: 8 (over z, y), cols: 2 (over core).
Axes of the slice: x: 2, y: 2, z: 4, core: 2. Of those that a mesh axis runs over, the one named last changes fastest.
Arguments:
- left_feat: bfloat16 [32, 512, 256], P(('pairs', 'rows'), 'cols'), parts along dimension 0, may hold values from -6 to 6
- right_feat: bfloat16 [32, 512, 256], P(('pairs', 'rows'), 'cols'), parts along dimension 0, may hold values from -6 to 6
- block_list: int32 [16, 8, 2], P(('pairs', 'rows'), 'cols'), parts along dimension 0, may hold values from 0 to 1, as said below
- block_count: int32 [16, 8], P(('pairs', 'rows'), 'cols'), parts along dimension 0, may hold values from 1 to 2
- spatial_first: bfloat16 [3, 3, 16, 16], replicated, may hold values from -0.75 to 0.75
- spatial_second: bfloat16 [3, 3, 16, 16], replicated, may hold values from -0.75 to 0.75
- disparity_weight: bfloat16 [17, 16], replicated, may hold values from -0.5 to 0.5
Outputs:
- cost: float32 [32, 512, 256], P(('pairs', 'rows'), 'cols'), parts along dimension 0
There are 2 independent parts, one for each index of `pairs`. A program takes and returns all parts, laid end to end along the dimension named above; an argument that names none is the same for every part. Nothing has to cross between parts.
Inputs may be any that keep to these rules, and one draw needn't show every extreme that they name: `block_list`: for each tile the 2 entries are different block numbers; entries in slots at or past the tile's block_count are not listed.
All inputs are finite; a program needn't handle non-finite values.
Results may differ from a plain program's by a relative error of at most 0.0059.
Values may be sent and summed in bfloat16 or wider, within the bound.
A program may use at most 128 MiB of HBM per device.

v0:
```python
import jax
import jax.numpy as jnp
from jax import lax
from jax.experimental import pallas as pl
from jax.experimental.pallas import tpu as pltpu
from jax.sharding import PartitionSpec as P

C = 256
G = 16
CG = C // G
DB = 128
NBLK = 2
ND = DB * NBLK
TILE = 64
TAPS = 17
BLK = 128
RIM = 2
P1 = 6
P2 = 8
PAD = 16
MESH = pl.DeviceIdType.MESH


def window_weights(taps, wide):
    lane = lax.broadcasted_iota(jnp.int32, (G, 4 * BLK), 1)
    group = lax.broadcasted_iota(jnp.int32, (G, 4 * BLK), 0)
    base = jnp.zeros((G, 4 * BLK), jnp.float32)
    for i in range(3):
        for j in range(3):
            pick = (lane == group + (i * wide + j) * G).astype(jnp.float32).astype(jnp.bfloat16)
            base = base + jnp.dot(taps[3 * i + j], pick, preferred_element_type=jnp.float32)
    return base


def kernel(flags, left, right, act, sf, ss, td, out, l32, rt, a_buf, vol, h1, h2, w1, w2, a32):
    ext_rows, ext_cols, _ = left.shape
    strip = ext_cols - 2 * PAD
    out_rows = ext_rows - 2 * RIM
    base = window_weights(sf, P1 + 2)
    for i in range(2):
        for j in range(P1):
            move = (i * (P1 + 2) + j) * G
            piece = pltpu.roll(base, move, 1) if move else base
            at = (i * P1 + j) * G
            w1[at : at + G, :] = piece.astype(jnp.bfloat16)
    base = window_weights(ss, P2 + 2)
    for j in range(P2):
        piece = pltpu.roll(base, j * G, 1) if j else base
        w2[j * G : (j + 1) * G, :] = piece.astype(jnp.bfloat16)
    to = lax.broadcasted_iota(jnp.int32, (P2 * G, P2 * G), 0)
    at = lax.broadcasted_iota(jnp.int32, (P2 * G, P2 * G), 1)
    order = (at == (to % P2) * G + to // P2).astype(jnp.float32).astype(jnp.bfloat16)
    w2[...] = jnp.dot(order, w2[...], preferred_element_type=jnp.float32).astype(jnp.bfloat16)
    tiles = strip // BLK
    back = ND // BLK
    blocks = right.shape[1] // BLK
    chunk = 32
    chan = lax.broadcasted_iota(jnp.int32, (G, C), 1) // CG
    grp = lax.broadcasted_iota(jnp.int32, (G, C), 0)
    diag = (chan == grp).astype(jnp.float32).astype(jnp.bfloat16)

    def fill(y, x_ext, count, slot):
        for i in range(count):
            row = jnp.broadcast_to(l32[pl.ds(x_ext + (PAD - RIM) + i, 1), :], (G, C)).astype(jnp.bfloat16)
            a_buf[slot + i * G : slot + (i + 1) * G, :] = row * diag

    def emit(y, x_ext, prod, i, xi, scale):
        piece = prod[i * G : (i + 1) * G, 1 + xi : 1 + xi + ND]
        vol[y, pl.ds(pl.multiple_of((x_ext + i) * G, G), G), :] = piece * scale

    def row_step(y, carry):
        l32[...] = left[y].astype(jnp.float32)
        for b in range(blocks):
            rt[:, b * BLK : (b + 1) * BLK] = right[y, b * BLK : (b + 1) * BLK, :].T

        for side in range(3):
            a32[side] = act[side, y].astype(jnp.float32)

        def scale_of(side, tile):
            return jnp.broadcast_to(a32[side, pl.ds(tile, 1), :], (G, ND)).astype(jnp.bfloat16)

        def tile_step(t, carry):
            window = rt[:, pl.ds(pl.multiple_of((t + 1) * BLK, BLK), BLK + ND)]
            for half in range(BLK // TILE):
                scale = scale_of(1, t * (BLK // TILE) + half)
                for c in range(TILE // chunk):
                    xi = half * TILE + c * chunk
                    fill(y, RIM + t * BLK + xi, chunk, 0)
                    prod = jnp.dot(
                        a_buf[0 : chunk * G, :], window, preferred_element_type=jnp.float32
                    ).astype(jnp.bfloat16)
                    for i in range(chunk):
                        emit(y, RIM + t * BLK + xi, prod, i, xi + i, scale)
            return carry

        lax.fori_loop(0, tiles, tile_step, 0)
        fill(y, 0, RIM, 0)
        prod = jnp.dot(
            a_buf[0 : RIM * G, :], rt[:, 0 : BLK + ND], preferred_element_type=jnp.float32
        ).astype(jnp.bfloat16)
        scale = scale_of(0, strip // TILE - 1)
        for i in range(RIM):
            emit(y, 0, prod, i, BLK - RIM + i, scale)
        fill(y, RIM + strip, RIM, 0)
        first = (1 + tiles) * BLK
        prod = jnp.dot(
            a_buf[0 : RIM * G, :],
            rt[:, first : first + BLK + ND],
            preferred_element_type=jnp.float32,
        ).astype(jnp.bfloat16)
        scale = scale_of(2, 0)
        for i in range(RIM):
            emit(y, RIM + strip, prod, i, i, scale)
        return carry

    lax.fori_loop(0, ext_rows, row_step, 0)

    def conv1_step(w, carry):
        at = pl.multiple_of(w * (P1 * G), P1 * G)
        for yp in range((out_rows + 2) // 2):
            x = jnp.concatenate(
                [vol[2 * yp + r, pl.ds(at, (P1 + 2) * G), :] for r in range(4)], axis=0
            )
            y = jnp.dot(w1[...], x, preferred_element_type=jnp.float32)
            y = jnp.maximum(y, 0.0).astype(jnp.bfloat16)
            for r in range(2):
                h1[2 * yp + r, pl.ds(at, P1 * G), :] = y[r * P1 * G : (r + 1) * P1 * G, :]
        return carry

    lax.fori_loop(0, (strip + 2) // P1, conv1_step, 0)

    span = (strip + 2) * G

    @pl.when(flags[0] == 0)
    def _():
        h1[0, 0:span, :] = jnp.zeros((span, ND), jnp.bfloat16)

    @pl.when(flags[1] == 0)
    def _():
        h1[out_rows + 1, 0:span, :] = jnp.zeros((span, ND), jnp.bfloat16)

    @pl.when(flags[2] == 0)
    def _():
        h1[:, 0:G, :] = jnp.zeros((out_rows + 2, G, ND), jnp.bfloat16)

    @pl.when(flags[3] == 0)
    def _():
        h1[:, span - G : span, :] = jnp.zeros((out_rows + 2, G, ND), jnp.bfloat16)

    def conv2_step(w, carry):
        for y in range(out_rows):
            halves = []
            for h in range(2):
                at = pl.multiple_of((w * 2 + h) * (P2 * G), P2 * G)
                x = jnp.concatenate(
                    [h1[y + r, pl.ds(at, (P2 + 2) * G), :] for r in range(3)], axis=0
                )
                r = jnp.dot(w2[:, 0 : 3 * (P2 + 2) * G], x, preferred_element_type=jnp.float32)
                halves.append(jnp.maximum(r, 0.0))
            px = pl.multiple_of(y * strip + w * (2 * P2), 2 * P2)
            for g in range(G):
                both = jnp.concatenate([q[g * P2 : (g + 1) * P2] for q in halves], axis=0)
                h2[g, pl.ds(px, 2 * P2), :] = both.astype(jnp.bfloat16)
        return carry

    lax.fori_loop(0, strip // (2 * P2), conv2_step, 0)

    for y in range(out_rows):
        total = None
        for g in range(G):
            part = jnp.dot(
                h2[g, y * strip : (y + 1) * strip, :], td[g], preferred_element_type=jnp.float32
            )
            total = part if total is None else total + part
        out[y] = total


def halo_kernel(dw, left, right, act, lx, rx, ax, td, send, recv, local, row_sem, row_recv):
    rows, strip, _ = left.shape
    band, bands = lax.axis_index("rows"), lax.axis_size("rows")
    col, cols = lax.axis_index("cols"), lax.axis_size("cols")
    own = slice(RIM, RIM + rows)
    r0 = BLK + ND
    has_above, has_below = band > 0, band < bands - 1
    has_prev, has_next = col > 0, col < cols - 1

    barrier = pltpu.get_barrier_semaphore()

    def greet(there, device):
        @pl.when(there)
        def _():
            pl.semaphore_signal(barrier, inc=1, device_id=device, device_id_type=MESH)

    greet(has_above, {"rows": band - 1})
    greet(has_below, {"rows": band + 1})
    greet(has_prev, {"cols": col - 1})
    greet(has_next, {"cols": col + 1})
    sides = (has_above, has_below, has_prev, has_next)
    pl.semaphore_wait(barrier, sum(there.astype(jnp.int32) for there in sides))

    def row_copies(device, first, slot):
        pairs = (
            (left, lx.at[first : first + rows, PAD : PAD + strip]),
            (right, rx.at[first : first + rows, r0 : r0 + strip]),
            (act, ax.at[1, first : first + rows]),
        )
        return [
            pltpu.make_async_remote_copy(
                src_ref=a, dst_ref=b, send_sem=row_sem.at[slot, i], recv_sem=row_recv.at[slot, i],
                device_id=device, device_id_type=MESH,
            )
            for i, (a, b) in enumerate(pairs)
        ]

    def col_copies(forward, part):
        at = slice(part * RIM, part * RIM + RIM)
        if part == 1:
            srcs = (left, right, act)
        else:
            srcs = (
                lx.at[at, PAD : PAD + strip], rx.at[at, r0 : r0 + strip], ax.at[1, at],
            )
        l_src, r_src, a_src = srcs
        if forward:
            pairs = (
                (l_src.at[:, strip - PAD : strip], lx.at[at, 0:PAD]),
                (r_src, rx.at[at, BLK : BLK + strip]),
                (a_src, ax.at[0, at]),
            )
        else:
            pairs = (
                (l_src.at[:, 0:PAD], lx.at[at, PAD + strip : 2 * PAD + strip]),
                (r_src.at[:, 0:PAD], rx.at[at, r0 + strip : r0 + strip + PAD]),
                (a_src, ax.at[2, at]),
            )
        slot = (0 if forward else 3) + part
        device = {"cols": col + 1 if forward else col - 1}
        return [
            pltpu.make_async_remote_copy(
                src_ref=a, dst_ref=b, send_sem=send.at[slot, i], recv_sem=recv.at[slot, i],
                device_id=device, device_id_type=MESH,
            )
            for i, (a, b) in enumerate(pairs)
        ]

    down = row_copies({"rows": band + 1}, 0, 0)
    up = row_copies({"rows": band - 1}, RIM + rows, 1)

    def when(there, action):
        @pl.when(there)
        def _():
            action()

    def start(copies):
        for q in copies:
            q.start()

    def got(copies):
        for q in copies:
            q.wait_recv()

    def sent(copies):
        for q in copies:
            q.wait_send()

    when(has_below, lambda: start(down))
    when(has_above, lambda: start(up))
    when(has_next, lambda: start(col_copies(True, 1)))
    when(has_prev, lambda: start(col_copies(False, 1)))
    mine = [
        pltpu.make_async_copy(left, lx.at[own, PAD : PAD + strip], local.at[0]),
        pltpu.make_async_copy(right, rx.at[own, r0 : r0 + strip], local.at[1]),
        pltpu.make_async_copy(act, ax.at[1, own], local.at[2]),
    ]
    start(mine)

    def zero(ref):
        ref[...] = jnp.zeros(ref.shape, ref.dtype)

    zero(rx.at[:, 0:BLK])
    zero(rx.at[:, r0 + strip + PAD : r0 + strip + BLK])

    def no_prev():
        zero(lx.at[own, 0:PAD])
        zero(rx.at[own, BLK:r0])
        zero(ax.at[0, own])

    def no_next():
        zero(lx.at[own, PAD + strip : 2 * PAD + strip])
        zero(rx.at[own, r0 + strip : r0 + strip + PAD])
        zero(ax.at[2, own])

    when(jnp.logical_not(has_prev), no_prev)
    when(jnp.logical_not(has_next), no_next)

    def no_rows(first):
        def run():
            at = slice(first, first + RIM)
            zero(lx.at[at])
            zero(rx.at[at, BLK : r0 + strip + PAD])
            for side in range(3):
                zero(ax.at[side, at])
        return run

    def halo_rims(first):
        def run():
            at = slice(first, first + RIM)

            def before():
                zero(lx.at[at, 0:PAD])
                zero(rx.at[at, BLK:r0])
                zero(ax.at[0, at])

            def after():
                zero(lx.at[at, PAD + strip : 2 * PAD + strip])
                zero(rx.at[at, r0 + strip : r0 + strip + PAD])
                zero(ax.at[2, at])

            when(jnp.logical_not(has_prev), before)
            when(jnp.logical_not(has_next), after)
        return run

    for there, first in ((has_above, 0), (has_below, RIM + rows)):
        when(jnp.logical_not(there), no_rows(first))
        when(there, halo_rims(first))

    def band_step(e, carry):
        at = e * PAD
        place = (
            ND - 1 + TAPS // 2 - at
            - lax.broadcasted_iota(jnp.int32, (PAD, ND), 0)
            - lax.broadcasted_iota(jnp.int32, (PAD, ND), 1)
        )
        for g in range(G):
            total = jnp.zeros((PAD, ND), jnp.float32)
            for k in range(TAPS):
                total = jnp.where(place == k, dw[k, g], total)
            td[g, pl.ds(pl.multiple_of(at, PAD), PAD), :] = total.astype(jnp.bfloat16)
        return carry

    lax.fori_loop(0, ND // PAD, band_step, 0)

    for there, copies, part in ((has_above, down, 0), (has_below, up, 2)):
        def forward(copies=copies, part=part):
            got(copies)
            when(has_next, lambda: start(col_copies(True, part)))
            when(has_prev, lambda: start(col_copies(False, part)))
        when(there, forward)

    for q in mine:
        q.wait()
    when(has_below, lambda: sent(down))
    when(has_above, lambda: sent(up))
    for there, part in ((None, 1), (has_above, 0), (has_below, 2)):
        def finish(part=part):
            when(has_next, lambda: sent(col_copies(True, part)))
            when(has_prev, lambda: sent(col_copies(False, part)))
            when(has_prev, lambda: got(col_copies(True, part)))
            when(has_next, lambda: got(col_copies(False, part)))
        if there is None:
            finish()
        else:
            when(there, finish)


def body(
    left_feat, right_feat, block_list, block_count, spatial_first, spatial_second, disparity_weight
):
    rows, strip, _ = left_feat.shape
    band, bands = lax.axis_index("rows"), lax.axis_size("rows")
    col, col_count = lax.axis_index("cols"), lax.axis_size("cols")
    if strip != ND or col_count > 2 or rows != RIM:
        raise ValueError("unsupported strip")
    tiles = strip // TILE
    n = rows + 2 * RIM

    live = jnp.arange(block_list.shape[2], dtype=jnp.int32) < block_count[0][:, None]
    lane_block = NBLK - 1 - jnp.arange(ND, dtype=jnp.int32) // DB
    hits = (block_list[0][:, :, None] == lane_block[None, None, :]) & live[:, :, None]
    act = jnp.where(jnp.any(hits, axis=1), CG ** (-0.5), 0.0).astype(jnp.bfloat16)
    act = jnp.broadcast_to(jnp.pad(act, ((0, PAD - tiles), (0, 0)))[None], (rows, PAD, ND))
    flags = jnp.stack([band > 0, band < bands - 1, col > 0, col < col_count - 1]).astype(jnp.int32)

    vmem = pl.BlockSpec(memory_space=pltpu.VMEM)
    smem = pl.BlockSpec(memory_space=pltpu.SMEM)
    right_len = BLK + ND + strip + BLK
    left, right, act, td = pl.pallas_call(
        halo_kernel,
        out_shape=(
            jax.ShapeDtypeStruct((n, strip + 2 * PAD, C), jnp.bfloat16),
            jax.ShapeDtypeStruct((n, right_len, C), jnp.bfloat16),
            jax.ShapeDtypeStruct((3, n, PAD, ND), jnp.bfloat16),
            jax.ShapeDtypeStruct((G, ND, ND), jnp.bfloat16),
        ),
        in_specs=[smem, vmem, vmem, vmem],
        out_specs=(vmem, vmem, vmem, vmem),
        scratch_shapes=[
            pltpu.SemaphoreType.DMA((6, 3)),
            pltpu.SemaphoreType.DMA((6, 3)),
            pltpu.SemaphoreType.DMA((3,)),
            pltpu.SemaphoreType.DMA((2, 3)),
            pltpu.SemaphoreType.DMA((2, 3)),
        ],
        compiler_params=pltpu.CompilerParams(collective_id=0, has_side_effects=True),
        name="halo",
    )(disparity_weight.astype(jnp.float32), left_feat, right_feat, act)

    return pl.pallas_call(
        kernel,
        out_shape=jax.ShapeDtypeStruct((rows, strip, ND), jnp.float32),
        in_specs=[smem] + [vmem] * 6,
        out_specs=vmem,
        scratch_shapes=[
            pltpu.VMEM((strip + 2 * PAD, C), jnp.float32),
            pltpu.VMEM((C, right_len), jnp.bfloat16),
            pltpu.VMEM((32 * G, C), jnp.bfloat16),
            pltpu.VMEM((n, (strip + 2 * RIM) * G, ND), jnp.bfloat16),
            pltpu.VMEM((rows + 2, (strip + 2) * G, ND), jnp.bfloat16),
            pltpu.VMEM((G, rows * strip, ND), jnp.bfloat16),
            pltpu.VMEM((2 * P1 * G, 4 * BLK), jnp.bfloat16),
            pltpu.VMEM((P2 * G, 4 * BLK), jnp.bfloat16),
            pltpu.VMEM((3, PAD, ND), jnp.float32),
        ],
        compiler_params=pltpu.CompilerParams(vmem_limit_bytes=56 * 1024 * 1024),
        name="cost_volume",
    )(
        flags, left, right, act,
        spatial_first.reshape(9, G, G), spatial_second.reshape(9, G, G), td,
    )


def solution(mesh):
    in_specs = (
        P(("pairs", "rows"), "cols", None),
        P(("pairs", "rows"), "cols", None),
        P(("pairs", "rows"), "cols", None),
        P(("pairs", "rows"), "cols"),
        P(),
        P(),
        P(),
    )
    out_specs = P(("pairs", "rows"), "cols", None)
    return jax.shard_map(body, mesh=mesh, in_specs=in_specs, out_specs=out_specs, check_vma=False)
```

profile of v0, /device:TPU:17, one launch (start us, length us, event | category | flops | bytes accessed | tf_op | source)
XLA Modules:
  0.0 106.6 jit_solution(6473519042051865425)
XLA Ops:
  0.0 0.6 add_convert_fusion.flags
  0.6 0.7 iota_compare_fusion
  1.2 0.8 and_reduce_fusion
  2.0 0.6 broadcast_in_dim.19.act
  2.6 1.4 %copy.11.dw = f32[17,16]{1,0:T(8,128)} copy(bf16[17,16]{0,1:T(8,128)(2,1)} %param.13) | data formatting | bytes 1632 | tf_op jit(solution)/shard_map/convert_element_type | solution.py:406
  4.0 32.1 %halo.1 = (bf16[6,288,256]{2,1,0:T(8,128)(2,1)}, bf16[6,768,256]{2,1,0:T(8,128)(2,1)}, bf16[3,6,16,256]{3,2,1,0:T(8,128)(2,1)}, bf16[16,256,256]{2,1,0:T(8,128)(2,1)}) custom-call(f32[17,16]{1,0:T(8,128)} %copy.11.dw, bf16[2,256,256]{2,1,0:T(8,128)(2,1)} %left.1, bf16[2,256,256]{2,1,0:T(8,128)(2,1)} %right.1, bf16[2,16,256]{2,1,0:T(8,128)(2,1)} %broadcast_in_dim.19.act), custom_call_target="tpu_custom_call" | custom-call | tf_op jit(solution)/shard_map/halo/pallas_call | solution.py:387
  36.1 70.5 %cost_volume.1 = f32[2,256,256]{2,1,0:T(8,128)} custom-call(s32[4]{0:T(128)} %add_convert_fusion.flags, bf16[6,288,256]{2,1,0:T(8,128)(2,1)} %get-tuple-element.9.left, bf16[6,768,256]{2,1,0:T(8,128)(2,1)} %get-tuple-element.10.right, bf16[3,6,16,256]{3,2,1,0:T(8,128)(2,1)} %get-tuple-element.11.act, bf16[9,16,16]{2,1,0:T(8,128)(2,1)} %bitcast.8, ...), custom_call_target="tpu_custom_call" | custom-call | tf_op jit(solution)/shard_map/cost_volume/pallas_call | solution.py:408
  (3 shorter events, 0.0 us)
where the time goes:
time: 107 us
  Pallas kernels  103 us (96%)
  other arithmetic  1.99 us (2%)
  local copies, waits for them, and re-layouts  1.98 us (2%)
    pallas_call x1, Pallas kernels, body(): pl.pallas_call(kernel, out_shape=jax.ShapeDtypeStruct((rows, strip, ND),...  70.5 us
    pallas_call x1, Pallas kernels, body(): pl.pallas_call(halo_kernel, out_shape=(jax.ShapeDtypeStruct((n, strip + 2...  32.1 us

commit v1 on v0

--- a/solution.py
+++ b/solution.py
@@ -65,7 +65,8 @@
             a_buf[slot + i * G : slot + (i + 1) * G, :] = row * diag
 
     def emit(y, x_ext, prod, i, xi, scale):
-        piece = prod[i * G : (i + 1) * G, 1 + xi : 1 + xi + ND]
+        wide = prod[i * G : (i + 1) * G, :]
+        piece = pltpu.roll(wide, wide.shape[1] - 1 - xi, 1)[:, :ND].astype(jnp.bfloat16)
         vol[y, pl.ds(pl.multiple_of((x_ext + i) * G, G), G), :] = piece * scale
 
     def row_step(y, carry):
@@ -85,10 +86,11 @@
                 scale = scale_of(1, t * (BLK // TILE) + half)
                 for c in range(TILE // chunk):
                     xi = half * TILE + c * chunk
-                    fill(y, RIM + t * BLK + xi, chunk, 0)
+                    slot = xi * G
+                    fill(y, RIM + t * BLK + xi, chunk, slot)
                     prod = jnp.dot(
-                        a_buf[0 : chunk * G, :], window, preferred_element_type=jnp.float32
-                    ).astype(jnp.bfloat16)
+                        a_buf[slot : slot + chunk * G, :], window, preferred_element_type=jnp.float32
+                    )
                     for i in range(chunk):
                         emit(y, RIM + t * BLK + xi, prod, i, xi + i, scale)
             return carry
@@ -97,7 +99,7 @@
         fill(y, 0, RIM, 0)
         prod = jnp.dot(
             a_buf[0 : RIM * G, :], rt[:, 0 : BLK + ND], preferred_element_type=jnp.float32
-        ).astype(jnp.bfloat16)
+        )
         scale = scale_of(0, strip // TILE - 1)
         for i in range(RIM):
             emit(y, 0, prod, i, BLK - RIM + i, scale)
@@ -107,7 +109,7 @@
             a_buf[0 : RIM * G, :],
             rt[:, first : first + BLK + ND],
             preferred_element_type=jnp.float32,
-        ).astype(jnp.bfloat16)
+        )
         scale = scale_of(2, 0)
         for i in range(RIM):
             emit(y, RIM + strip, prod, i, i, scale)
@@ -115,8 +117,8 @@
 
     lax.fori_loop(0, ext_rows, row_step, 0)
 
-    def conv1_step(w, carry):
-        at = pl.multiple_of(w * (P1 * G), P1 * G)
+    def conv1_window(w):
+        at = w * (P1 * G) if isinstance(w, int) else pl.multiple_of(w * (P1 * G), P1 * G)
         for yp in range((out_rows + 2) // 2):
             x = jnp.concatenate(
                 [vol[2 * yp + r, pl.ds(at, (P1 + 2) * G), :] for r in range(4)], axis=0
@@ -125,9 +127,16 @@
             y = jnp.maximum(y, 0.0).astype(jnp.bfloat16)
             for r in range(2):
                 h1[2 * yp + r, pl.ds(at, P1 * G), :] = y[r * P1 * G : (r + 1) * P1 * G, :]
+
+    def conv1_step(q, carry):
+        for i in range(3):
+            conv1_window(q * 3 + i)
         return carry
 
-    lax.fori_loop(0, (strip + 2) // P1, conv1_step, 0)
+    windows = (strip + 2) // P1
+    lax.fori_loop(0, windows // 3, conv1_step, 0)
+    for w in range(windows // 3 * 3, windows):
+        conv1_window(w)
 
     span = (strip + 2) * G
 
@@ -147,7 +156,7 @@
     def _():
         h1[:, span - G : span, :] = jnp.zeros((out_rows + 2, G, ND), jnp.bfloat16)
 
-    def conv2_step(w, carry):
+    def conv2_window(w):
         for y in range(out_rows):
             halves = []
             for h in range(2):
@@ -161,9 +170,13 @@
             for g in range(G):
                 both = jnp.concatenate([q[g * P2 : (g + 1) * P2] for q in halves], axis=0)
                 h2[g, pl.ds(px, 2 * P2), :] = both.astype(jnp.bfloat16)
+
+    def conv2_step(q, carry):
+        for i in range(2):
+            conv2_window(q * 2 + i)
         return carry
 
-    lax.fori_loop(0, strip // (2 * P2), conv2_step, 0)
+    lax.fori_loop(0, strip // (4 * P2), conv2_step, 0)
 
     for y in range(out_rows):
         total = None
@@ -324,21 +337,30 @@
         when(jnp.logical_not(there), no_rows(first))
         when(there, halo_rims(first))
 
-    def band_step(e, carry):
-        at = e * PAD
-        place = (
-            ND - 1 + TAPS // 2 - at
-            - lax.broadcasted_iota(jnp.int32, (PAD, ND), 0)
-            - lax.broadcasted_iota(jnp.int32, (PAD, ND), 1)
-        )
-        for g in range(G):
-            total = jnp.zeros((PAD, ND), jnp.float32)
-            for k in range(TAPS):
-                total = jnp.where(place == k, dw[k, g], total)
-            td[g, pl.ds(pl.multiple_of(at, PAD), PAD), :] = total.astype(jnp.bfloat16)
-        return carry
-
-    lax.fori_loop(0, ND // PAD, band_step, 0)
+    def band_steps(lane, first, last):
+        def step(e, carry):
+            at = e * PAD
+            place = (
+                ND - 1 + TAPS // 2 - lane - at
+                - lax.broadcasted_iota(jnp.int32, (PAD, BLK), 0)
+                - lax.broadcasted_iota(jnp.int32, (PAD, BLK), 1)
+            )
+            for g in range(G):
+                total = jnp.zeros((PAD, BLK), jnp.float32)
+                for k in range(TAPS):
+                    total = jnp.where(place == k, dw[k, g], total)
+                td[g, pl.ds(pl.multiple_of(at, PAD), PAD), lane : lane + BLK] = total.astype(
+                    jnp.bfloat16
+                )
+            return carry
+
+        lax.fori_loop(first, last, step, 0)
+
+    half = BLK // PAD
+    td[:, 0 : BLK - PAD, 0:BLK] = jnp.zeros((G, BLK - PAD, BLK), jnp.bfloat16)
+    td[:, BLK + PAD : ND, BLK:ND] = jnp.zeros((G, BLK - PAD, BLK), jnp.bfloat16)
+    band_steps(0, half - 1, 2 * half)
+    band_steps(BLK, 0, half + 1)
 
     for there, copies, part in ((has_above, down, 0), (has_below, up, 2)):
         def forward(copies=copies, part=part):
@@ -413,7 +435,7 @@
         scratch_shapes=[
             pltpu.VMEM((strip + 2 * PAD, C), jnp.float32),
             pltpu.VMEM((C, right_len), jnp.bfloat16),
-            pltpu.VMEM((32 * G, C), jnp.bfloat16),
+            pltpu.VMEM((BLK * G, C), jnp.bfloat16),
             pltpu.VMEM((n, (strip + 2 * RIM) * G, ND), jnp.bfloat16),
             pltpu.VMEM((rows + 2, (strip + 2) * G, ND), jnp.bfloat16),
             pltpu.VMEM((G, rows * strip, ND), jnp.bfloat16),

time: 107 us -> 65.3 us (0.61)
  Pallas kernels: 103 us -> 61.1 us
    pallas_call x1, Pallas kernels: 70.5 us -> 28.9 us  [body(): pl.pallas_call(kernel, out_shape=jax.ShapeDtypeStruct((rows, strip, ND),...]
where the time goes in v1:
time: 65.3 us; the launch traced here: 65 us
  Pallas kernels  61.1 us (94%)
  other arithmetic  1.99 us (3%)
  local copies, waits for them, and re-layouts  1.98 us (3%)
    pallas_call x1, Pallas kernels, body(): pl.pallas_call(halo_kernel, out_shape=(jax.ShapeDtypeStruct((n, strip + 2...  32.1 us
    pallas_call x1, Pallas kernels, body(): pl.pallas_call(kernel, out_shape=jax.ShapeDtypeStruct((rows, strip, ND),...  28.9 us
    convert_element_type x1, local copies, waits for them, and re-layouts, body(): disparity_weight.astype(jnp.float32)  1.36 us

profile of v1, /device:TPU:17, one launch (start us, length us, event | category | flops | bytes accessed | tf_op | source)
XLA Modules:
  0.0 65.0 jit_solution(17746199561392345815)
XLA Ops:
  0.0 0.6 add_convert_fusion.flags
  0.6 0.7 %iota_compare_fusion = pred[4,2]{0,1:T(4,128)(4,1)S(1)} fusion(s32[4]{0:T(128)} %bitcast.11), kind=kLoop, calls=%fused_computation.8 | loop fusion | flops 8 | bytes 24 | tf_op jit(solution)/shard_map/lt | solution.py:399
  1.2 0.8 %and_reduce_fusion = pred[4,256]{1,0:T(4,128)(4,1)S(1)} fusion(s32[256]{0:T(256)S(1)} %fusion, s32[4,2]{0,1:T(2,128)} %bitcast.10, pred[4,2]{0,1:T(4,128)(4,1)S(1)} %iota_compare_fusion), kind=kLoop, calls=%fused_computation | loop fusion | flops 5120 | bytes 2088 | tf_op jit(solution)/shard_map/reduce_or | solution.py:402
  2.0 0.6 broadcast_in_dim.19.act
  2.6 1.4 %copy.11.dw = f32[17,16]{1,0:T(8,128)} copy(bf16[17,16]{0,1:T(8,128)(2,1)} %param.13) | data formatting | bytes 1632 | tf_op jit(solution)/shard_map/convert_element_type | solution.py:428
  4.0 32.1 %halo.1 = (bf16[6,288,256]{2,1,0:T(8,128)(2,1)}, bf16[6,768,256]{2,1,0:T(8,128)(2,1)}, bf16[3,6,16,256]{3,2,1,0:T(8,128)(2,1)}, bf16[16,256,256]{2,1,0:T(8,128)(2,1)}) custom-call(f32[17,16]{1,0:T(8,128)} %copy.11.dw, bf16[2,256,256]{2,1,0:T(8,128)(2,1)} %left.1, bf16[2,256,256]{2,1,0:T(8,128)(2,1)} %right.1, bf16[2,16,256]{2,1,0:T(8,128)(2,1)} %broadcast_in_dim.19.act), custom_call_target="tpu_custom_call" | custom-call | tf_op jit(solution)/shard_map/halo/pallas_call | solution.py:409
  36.1 28.9 %cost_volume.1 = f32[2,256,256]{2,1,0:T(8,128)} custom-call(s32[4]{0:T(128)} %add_convert_fusion.flags, bf16[6,288,256]{2,1,0:T(8,128)(2,1)} %get-tuple-element.9.left, bf16[6,768,256]{2,1,0:T(8,128)(2,1)} %get-tuple-element.10.right, bf16[3,6,16,256]{3,2,1,0:T(8,128)(2,1)} %get-tuple-element.11.act, bf16[9,16,16]{2,1,0:T(8,128)(2,1)} %bitcast.8, ...), custom_call_target="tpu_custom_call" | custom-call | tf_op jit(solution)/shard_map/cost_volume/pallas_call | solution.py:430
  (3 shorter events, 0.0 us)

commit v2 on v1

--- a/solution.py
+++ b/solution.py
@@ -32,10 +32,7 @@
     return base
 
 
-def kernel(flags, left, right, act, sf, ss, td, out, l32, rt, a_buf, vol, h1, h2, w1, w2, a32):
-    ext_rows, ext_cols, _ = left.shape
-    strip = ext_cols - 2 * PAD
-    out_rows = ext_rows - 2 * RIM
+def weights(sf, ss, w1, w2):
     base = window_weights(sf, P1 + 2)
     for i in range(2):
         for j in range(P1):
@@ -51,8 +48,11 @@
     at = lax.broadcasted_iota(jnp.int32, (P2 * G, P2 * G), 1)
     order = (at == (to % P2) * G + to // P2).astype(jnp.float32).astype(jnp.bfloat16)
     w2[...] = jnp.dot(order, w2[...], preferred_element_type=jnp.float32).astype(jnp.bfloat16)
+
+
+def correlate(steps, row_of, left, right, act, l32, rt, a_buf, vol, a32):
+    strip = left.shape[1] - 2 * PAD
     tiles = strip // BLK
-    back = ND // BLK
     blocks = right.shape[1] // BLK
     chunk = 32
     chan = lax.broadcasted_iota(jnp.int32, (G, C), 1) // CG
@@ -69,7 +69,8 @@
         piece = pltpu.roll(wide, wide.shape[1] - 1 - xi, 1)[:, :ND].astype(jnp.bfloat16)
         vol[y, pl.ds(pl.multiple_of((x_ext + i) * G, G), G), :] = piece * scale
 
-    def row_step(y, carry):
+    def row_step(step, carry):
+        y = row_of(step)
         l32[...] = left[y].astype(jnp.float32)
         for b in range(blocks):
             rt[:, b * BLK : (b + 1) * BLK] = right[y, b * BLK : (b + 1) * BLK, :].T
@@ -115,7 +116,11 @@
             emit(y, RIM + strip, prod, i, i, scale)
         return carry
 
-    lax.fori_loop(0, ext_rows, row_step, 0)
+    lax.fori_loop(0, steps, row_step, 0)
+
+
+def convolve(sides, td, out, vol, h1, h2, w1, w2):
+    out_rows, strip, _ = out.shape
 
     def conv1_window(w):
         at = w * (P1 * G) if isinstance(w, int) else pl.multiple_of(w * (P1 * G), P1 * G)
@@ -140,19 +145,19 @@
 
     span = (strip + 2) * G
 
-    @pl.when(flags[0] == 0)
+    @pl.when(jnp.logical_not(sides[0]))
     def _():
         h1[0, 0:span, :] = jnp.zeros((span, ND), jnp.bfloat16)
 
-    @pl.when(flags[1] == 0)
+    @pl.when(jnp.logical_not(sides[1]))
     def _():
         h1[out_rows + 1, 0:span, :] = jnp.zeros((span, ND), jnp.bfloat16)
 
-    @pl.when(flags[2] == 0)
+    @pl.when(jnp.logical_not(sides[2]))
     def _():
         h1[:, 0:G, :] = jnp.zeros((out_rows + 2, G, ND), jnp.bfloat16)
 
-    @pl.when(flags[3] == 0)
+    @pl.when(jnp.logical_not(sides[3]))
     def _():
         h1[:, span - G : span, :] = jnp.zeros((out_rows + 2, G, ND), jnp.bfloat16)
 
@@ -188,7 +193,10 @@
         out[y] = total
 
 
-def halo_kernel(dw, left, right, act, lx, rx, ax, td, send, recv, local, row_sem, row_recv):
+def kernel(
+    dw, left, right, act, sf, ss, out, lx, rx, ax, td, l32, rt, a_buf, vol, h1, h2, w1, w2, a32,
+    send, recv, local, row_sem, row_recv,
+):
     rows, strip, _ = left.shape
     band, bands = lax.axis_index("rows"), lax.axis_size("rows")
     col, cols = lax.axis_index("cols"), lax.axis_size("cols")
@@ -362,36 +370,46 @@
     band_steps(0, half - 1, 2 * half)
     band_steps(BLK, 0, half + 1)
 
-    for there, copies, part in ((has_above, down, 0), (has_below, up, 2)):
+    weights(sf, ss, w1, w2)
+
+    def arrived(part):
+        when(has_prev, lambda: got(col_copies(True, part)))
+        when(has_next, lambda: got(col_copies(False, part)))
+
+    def left_off(part):
+        when(has_next, lambda: sent(col_copies(True, part)))
+        when(has_prev, lambda: sent(col_copies(False, part)))
+
+    for q in mine:
+        q.wait()
+    arrived(1)
+    work = (lx, rx, ax, l32, rt, a_buf, vol, a32)
+    correlate(rows, lambda i: i + RIM, *work)
+
+    halves = ((has_above, down, 0), (has_below, up, 2))
+    for there, copies, part in halves:
         def forward(copies=copies, part=part):
             got(copies)
             when(has_next, lambda: start(col_copies(True, part)))
             when(has_prev, lambda: start(col_copies(False, part)))
         when(there, forward)
-
-    for q in mine:
-        q.wait()
+    for there, copies, part in halves:
+        when(there, lambda part=part: arrived(part))
+    correlate(2 * RIM, lambda i: i + (i // RIM) * rows, *work)
+
     when(has_below, lambda: sent(down))
     when(has_above, lambda: sent(up))
-    for there, part in ((None, 1), (has_above, 0), (has_below, 2)):
-        def finish(part=part):
-            when(has_next, lambda: sent(col_copies(True, part)))
-            when(has_prev, lambda: sent(col_copies(False, part)))
-            when(has_prev, lambda: got(col_copies(True, part)))
-            when(has_next, lambda: got(col_copies(False, part)))
-        if there is None:
-            finish()
-        else:
-            when(there, finish)
+    left_off(1)
+    for there, copies, part in halves:
+        when(there, lambda part=part: left_off(part))
+    convolve(sides, td, out, vol, h1, h2, w1, w2)
 
 
 def body(
     left_feat, right_feat, block_list, block_count, spatial_first, spatial_second, disparity_weight
 ):
     rows, strip, _ = left_feat.shape
-    band, bands = lax.axis_index("rows"), lax.axis_size("rows")
-    col, col_count = lax.axis_index("cols"), lax.axis_size("cols")
-    if strip != ND or col_count > 2 or rows != RIM:
+    if strip != ND or lax.axis_size("cols") > 2 or rows != RIM:
         raise ValueError("unsupported strip")
     tiles = strip // TILE
     n = rows + 2 * RIM
@@ -401,38 +419,20 @@
     hits = (block_list[0][:, :, None] == lane_block[None, None, :]) & live[:, :, None]
     act = jnp.where(jnp.any(hits, axis=1), CG ** (-0.5), 0.0).astype(jnp.bfloat16)
     act = jnp.broadcast_to(jnp.pad(act, ((0, PAD - tiles), (0, 0)))[None], (rows, PAD, ND))
-    flags = jnp.stack([band > 0, band < bands - 1, col > 0, col < col_count - 1]).astype(jnp.int32)
 
     vmem = pl.BlockSpec(memory_space=pltpu.VMEM)
     smem = pl.BlockSpec(memory_space=pltpu.SMEM)
     right_len = BLK + ND + strip + BLK
-    left, right, act, td = pl.pallas_call(
-        halo_kernel,
-        out_shape=(
-            jax.ShapeDtypeStruct((n, strip + 2 * PAD, C), jnp.bfloat16),
-            jax.ShapeDtypeStruct((n, right_len, C), jnp.bfloat16),
-            jax.ShapeDtypeStruct((3, n, PAD, ND), jnp.bfloat16),
-            jax.ShapeDtypeStruct((G, ND, ND), jnp.bfloat16),
-        ),
-        in_specs=[smem, vmem, vmem, vmem],
-        out_specs=(vmem, vmem, vmem, vmem),
-        scratch_shapes=[
-            pltpu.SemaphoreType.DMA((6, 3)),
-            pltpu.SemaphoreType.DMA((6, 3)),
-            pltpu.SemaphoreType.DMA((3,)),
-            pltpu.SemaphoreType.DMA((2, 3)),
-            pltpu.SemaphoreType.DMA((2, 3)),
-        ],
-        compiler_params=pltpu.CompilerParams(collective_id=0, has_side_effects=True),
-        name="halo",
-    )(disparity_weight.astype(jnp.float32), left_feat, right_feat, act)
-
     return pl.pallas_call(
         kernel,
         out_shape=jax.ShapeDtypeStruct((rows, strip, ND), jnp.float32),
-        in_specs=[smem] + [vmem] * 6,
+        in_specs=[smem] + [vmem] * 5,
         out_specs=vmem,
         scratch_shapes=[
+            pltpu.VMEM((n, strip + 2 * PAD, C), jnp.bfloat16),
+            pltpu.VMEM((n, right_len, C), jnp.bfloat16),
+            pltpu.VMEM((3, n, PAD, ND), jnp.bfloat16),
+            pltpu.VMEM((G, ND, ND), jnp.bfloat16),
             pltpu.VMEM((strip + 2 * PAD, C), jnp.float32),
             pltpu.VMEM((C, right_len), jnp.bfloat16),
             pltpu.VMEM((BLK * G, C), jnp.bfloat16),
@@ -442,12 +442,19 @@
             pltpu.VMEM((2 * P1 * G, 4 * BLK), jnp.bfloat16),
             pltpu.VMEM((P2 * G, 4 * BLK), jnp.bfloat16),
             pltpu.VMEM((3, PAD, ND), jnp.float32),
+            pltpu.SemaphoreType.DMA((6, 3)),
+            pltpu.SemaphoreType.DMA((6, 3)),
+            pltpu.SemaphoreType.DMA((3,)),
+            pltpu.SemaphoreType.DMA((2, 3)),
+            pltpu.SemaphoreType.DMA((2, 3)),
         ],
-        compiler_params=pltpu.CompilerParams(vmem_limit_bytes=56 * 1024 * 1024),
+        compiler_params=pltpu.CompilerParams(
+            collective_id=0, has_side_effects=True, vmem_limit_bytes=56 * 1024 * 1024
+        ),
         name="cost_volume",
     )(
-        flags, left, right, act,
-        spatial_first.reshape(9, G, G), spatial_second.reshape(9, G, G), td,
+        disparity_weight.astype(jnp.float32), left_feat, right_feat, act,
+        spatial_first.reshape(9, G, G), spatial_second.reshape(9, G, G),
     )
 
 

time: 65.3 us -> 56 us (0.86)
  Pallas kernels: 61.1 us -> 51.1 us
  local copies, waits for them, and re-layouts: 1.98 us -> 4.56 us
  other arithmetic: 1.99 us -> 0.1 us
    pallas_call x1 -> x0, Pallas kernels: 32.1 us -> none  [body(): pl.pallas_call(halo_kernel, out_shape=(jax.ShapeDtypeStruct((n, strip + 2...]
    pallas_call x1, Pallas kernels: 28.9 us -> 51.1 us  [body(): pl.pallas_call(kernel, out_shape=jax.ShapeDtypeStruct((rows, strip, ND),...]
    unnamed x0 -> x7, local copies, waits for them, and re-layouts: none -> 3.27 us
    convert_element_type x1, local copies, waits for them, and re-layouts: 1.36 us -> 0.68 us  [body(): disparity_weight.astype(jnp.float32)]
    reduce_or x1, other arithmetic: 0.76 us -> 0.08 us  [body(): jnp.any(hits, axis=1)]
    lt x1, other arithmetic: 0.66 us -> 0.01 us  [body(): jnp.arange(block_list.shape[2], dtype=jnp.int32) < block_count[0][:, None]]
where the time goes in v2:
time: 56 us; the launch traced here: 55.8 us
  Pallas kernels  51.1 us (91%)
  local copies, waits for them, and re-layouts  4.56 us (8%)
    pallas_call x1, Pallas kernels, body(): pl.pallas_call(kernel, out_shape=jax.ShapeDtypeStruct((rows, strip, ND),...  51.1 us
    unnamed x7, local copies, waits for them, and re-layouts  3.27 us

profile of v2, /device:TPU:17, one launch (start us, length us, event | category | flops | bytes accessed | tf_op | source)
XLA Modules:
  0.0 55.8 jit_solution(4153753110260854635)
XLA Ops:
  0.0 0.0 copy-start.2
  0.0 0.7 %copy-done.2 = s32[1,4]{1,0:T(1,128)S(1)} copy-done((s32[1,4]{1,0:T(1,128)S(1)}, s32[1,4]{1,0:T(1,128)}, u32[]{:S(2)}) %copy-start.2) | copy-done | bytes 40
  0.7 0.0 copy-start.1
  0.7 0.7 %copy-done.1 = s32[1,4,2]{1,2,0:T(2,128)S(1)} copy-done((s32[1,4,2]{1,2,0:T(2,128)S(1)}, s32[1,4,2]{1,2,0:T(2,128)}, u32[]{:S(2)}) %copy-start.1) | copy-done | bytes 56
  1.3 0.1 and_reduce_fusion
  1.4 0.0 copy-start
  1.5 0.6 %broadcast_in_dim.19.act = bf16[2,16,256]{2,1,0:T(8,128)(2,1)} broadcast(bf16[16,256]{1,0:T(8,128)(2,1)S(1)} %pad.4), dimensions={1,2} | broadcast | bytes 24576 | tf_op jit(solution)/shard_map/broadcast_in_dim | solution.py:421
  2.1 0.1 copy-done
  2.1 0.7 %copy.11.dw = f32[17,16]{1,0:T(8,128)} copy(bf16[17,16]{0,1:T(8,128)(2,1)S(1)} %copy-done) | data formatting | bytes 1632 | tf_op jit(solution)/shard_map/convert_element_type | solution.py:456
  2.8 51.1 %cost_volume.1 = f32[2,256,256]{2,1,0:T(8,128)} custom-call(f32[17,16]{1,0:T(8,128)} %copy.11.dw, bf16[2,256,256]{2,1,0:T(8,128)(2,1)} %left.1, bf16[2,256,256]{2,1,0:T(8,128)(2,1)} %right.1, bf16[2,16,256]{2,1,0:T(8,128)(2,1)} %broadcast_in_dim.19.act, bf16[9,16,16]{2,1,0:T(8,128)(2,1)} %bitcast.4, bf16[9,16,16]{2,1,0:T(8,128)(2,1)} %bitcast.5), custom_call_target="tpu_custom_call" | custom-call | tf_op jit(solution)/shard_map/cost_volume/pallas_call | solution.py:426
  53.9 1.9 %copy.13 = f32[2,256,256]{2,1,0:T(8,128)} copy(f32[2,256,256]{2,1,0:T(8,128)} %cost_volume.1) | data formatting | bytes 1048576
  (4 shorter events, 0.0 us)
Async XLA Ops:
  0.0 0.7 %copy-start.2 = (s32[1,4]{1,0:T(1,128)S(1)}, s32[1,4]{1,0:T(1,128)}, u32[]{:S(2)}) copy-start(s32[1,4]{1,0:T(1,128)} %param.10) | copy-start | bytes 52
  0.7 0.7 %copy-start.1 = (s32[1,4,2]{1,2,0:T(2,128)S(1)}, s32[1,4,2]{1,2,0:T(2,128)}, u32[]{:S(2)}) copy-start(s32[1,4,2]{1,2,0:T(2,128)} %param.9) | copy-start | bytes 100
  1.4 0.7 %copy-start = (bf16[17,16]{0,1:T(8,128)(2,1)S(1)}, bf16[17,16]{0,1:T(8,128)(2,1)}, u32[]{:S(2)}) copy-start(bf16[17,16]{0,1:T(8,128)(2,1)} %param.13) | copy-start | bytes 1636

commit v3 on v2

--- a/solution.py
+++ b/solution.py
@@ -219,11 +219,16 @@
     sides = (has_above, has_below, has_prev, has_next)
     pl.semaphore_wait(barrier, sum(there.astype(jnp.int32) for there in sides))
 
-    def row_copies(device, first, slot):
+    halo_rows = []
+    for i in range(RIM):
+        halo_rows += [RIM - 1 - i, RIM + rows + i]
+
+    def row_copies(device, src, dst, slot):
+        one, at = slice(src, src + 1), slice(dst, dst + 1)
         pairs = (
-            (left, lx.at[first : first + rows, PAD : PAD + strip]),
-            (right, rx.at[first : first + rows, r0 : r0 + strip]),
-            (act, ax.at[1, first : first + rows]),
+            (left.at[one], lx.at[at, PAD : PAD + strip]),
+            (right.at[one], rx.at[at, r0 : r0 + strip]),
+            (act.at[one], ax.at[1, at]),
         )
         return [
             pltpu.make_async_remote_copy(
@@ -234,8 +239,8 @@
         ]
 
     def col_copies(forward, part):
-        at = slice(part * RIM, part * RIM + RIM)
-        if part == 1:
+        at = own if part == 0 else slice(halo_rows[part - 1], halo_rows[part - 1] + 1)
+        if part == 0:
             srcs = (left, right, act)
         else:
             srcs = (
@@ -254,7 +259,7 @@
                 (r_src.at[:, 0:PAD], rx.at[at, r0 + strip : r0 + strip + PAD]),
                 (a_src, ax.at[2, at]),
             )
-        slot = (0 if forward else 3) + part
+        slot = (0 if forward else 1 + 2 * RIM) + part
         device = {"cols": col + 1 if forward else col - 1}
         return [
             pltpu.make_async_remote_copy(
@@ -264,8 +269,10 @@
             for i, (a, b) in enumerate(pairs)
         ]
 
-    down = row_copies({"rows": band + 1}, 0, 0)
-    up = row_copies({"rows": band - 1}, RIM + rows, 1)
+    down, up = [], []
+    for i in range(RIM):
+        down.append(row_copies({"rows": band + 1}, rows - 1 - i, RIM - 1 - i, 2 * i))
+        up.append(row_copies({"rows": band - 1}, i, RIM + rows + i, 2 * i + 1))
 
     def when(there, action):
         @pl.when(there)
@@ -284,10 +291,11 @@
         for q in copies:
             q.wait_send()
 
-    when(has_below, lambda: start(down))
-    when(has_above, lambda: start(up))
-    when(has_next, lambda: start(col_copies(True, 1)))
-    when(has_prev, lambda: start(col_copies(False, 1)))
+    for i in range(RIM):
+        when(has_below, lambda i=i: start(down[i]))
+        when(has_above, lambda i=i: start(up[i]))
+    when(has_next, lambda: start(col_copies(True, 0)))
+    when(has_prev, lambda: start(col_copies(False, 0)))
     mine = [
         pltpu.make_async_copy(left, lx.at[own, PAD : PAD + strip], local.at[0]),
         pltpu.make_async_copy(right, rx.at[own, r0 : r0 + strip], local.at[1]),
@@ -382,26 +390,29 @@
 
     for q in mine:
         q.wait()
-    arrived(1)
+    arrived(0)
     work = (lx, rx, ax, l32, rt, a_buf, vol, a32)
     correlate(rows, lambda i: i + RIM, *work)
 
-    halves = ((has_above, down, 0), (has_below, up, 2))
-    for there, copies, part in halves:
-        def forward(copies=copies, part=part):
-            got(copies)
-            when(has_next, lambda: start(col_copies(True, part)))
-            when(has_prev, lambda: start(col_copies(False, part)))
-        when(there, forward)
-    for there, copies, part in halves:
-        when(there, lambda part=part: arrived(part))
-    correlate(2 * RIM, lambda i: i + (i // RIM) * rows, *work)
-
-    when(has_below, lambda: sent(down))
-    when(has_above, lambda: sent(up))
-    left_off(1)
-    for there, copies, part in halves:
-        when(there, lambda part=part: left_off(part))
+    for i in range(RIM):
+        halves = ((has_above, down[i], 2 * i + 1), (has_below, up[i], 2 * i + 2))
+        for there, copies, part in halves:
+            def forward(copies=copies, part=part):
+                got(copies)
+                when(has_next, lambda: start(col_copies(True, part)))
+                when(has_prev, lambda: start(col_copies(False, part)))
+            when(there, forward)
+        for there, copies, part in halves:
+            when(there, lambda part=part: arrived(part))
+        near, far = halo_rows[2 * i], halo_rows[2 * i + 1]
+        correlate(2, lambda j, near=near, far=far: near + j * (far - near), *work)
+
+    left_off(0)
+    for i in range(RIM):
+        when(has_below, lambda i=i: sent(down[i]))
+        when(has_above, lambda i=i: sent(up[i]))
+        when(has_above, lambda i=i: left_off(2 * i + 1))
+        when(has_below, lambda i=i: left_off(2 * i + 2))
     convolve(sides, td, out, vol, h1, h2, w1, w2)
 
 
@@ -442,11 +453,11 @@
             pltpu.VMEM((2 * P1 * G, 4 * BLK), jnp.bfloat16),
             pltpu.VMEM((P2 * G, 4 * BLK), jnp.bfloat16),
             pltpu.VMEM((3, PAD, ND), jnp.float32),
-            pltpu.SemaphoreType.DMA((6, 3)),
-            pltpu.SemaphoreType.DMA((6, 3)),
+            pltpu.SemaphoreType.DMA((2 + 4 * RIM, 3)),
+            pltpu.SemaphoreType.DMA((2 + 4 * RIM, 3)),
             pltpu.SemaphoreType.DMA((3,)),
-            pltpu.SemaphoreType.DMA((2, 3)),
-            pltpu.SemaphoreType.DMA((2, 3)),
+            pltpu.SemaphoreType.DMA((2 * RIM, 3)),
+            pltpu.SemaphoreType.DMA((2 * RIM, 3)),
         ],
         compiler_params=pltpu.CompilerParams(
             collective_id=0, has_side_effects=True, vmem_limit_bytes=56 * 1024 * 1024

time: 56 us -> 51.8 us (0.925)
  Pallas kernels: 51.1 us -> 46.9 us
    pallas_call x1, Pallas kernels: 51.1 us -> 46.9 us  [body(): pl.pallas_call(kernel, out_shape=jax.ShapeDtypeStruct((rows, strip, ND),...]
where the time goes in v3:
time: 51.8 us; the launch traced here: 51.6 us
  Pallas kernels  46.9 us (91%)
  local copies, waits for them, and re-layouts  4.56 us (9%)
    pallas_call x1, Pallas kernels, body(): pl.pallas_call(kernel, out_shape=jax.ShapeDtypeStruct((rows, strip, ND),...  46.9 us
    unnamed x7, local copies, waits for them, and re-layouts  3.27 us

profile of v3, /device:TPU:17, one launch (start us, length us, event | category | flops | bytes accessed | tf_op | source)
XLA Modules:
  0.0 51.6 jit_solution(7061044433895010083)
XLA Ops:
  0.0 0.0 copy-start.2
  0.0 0.7 %copy-done.2 = s32[1,4]{1,0:T(1,128)S(1)} copy-done((s32[1,4]{1,0:T(1,128)S(1)}, s32[1,4]{1,0:T(1,128)}, u32[]{:S(2)}) %copy-start.2) | copy-done | bytes 40
  0.7 0.0 copy-start.1
  0.7 0.7 %copy-done.1 = s32[1,4,2]{1,2,0:T(2,128)S(1)} copy-done((s32[1,4,2]{1,2,0:T(2,128)S(1)}, s32[1,4,2]{1,2,0:T(2,128)}, u32[]{:S(2)}) %copy-start.1) | copy-done | bytes 56
  1.3 0.1 and_reduce_fusion
  1.4 0.0 copy-start
  1.5 0.6 %broadcast_in_dim.19.act = bf16[2,16,256]{2,1,0:T(8,128)(2,1)} broadcast(bf16[16,256]{1,0:T(8,128)(2,1)S(1)} %pad.4), dimensions={1,2} | broadcast | bytes 24576 | tf_op jit(solution)/shard_map/broadcast_in_dim | solution.py:432
  2.1 0.1 copy-done
  2.1 0.7 %copy.11.dw = f32[17,16]{1,0:T(8,128)} copy(bf16[17,16]{0,1:T(8,128)(2,1)S(1)} %copy-done) | data formatting | bytes 1632 | tf_op jit(solution)/shard_map/convert_element_type | solution.py:467
  2.8 46.9 %cost_volume.1 = f32[2,256,256]{2,1,0:T(8,128)} custom-call(f32[17,16]{1,0:T(8,128)} %copy.11.dw, bf16[2,256,256]{2,1,0:T(8,128)(2,1)} %left.1, bf16[2,256,256]{2,1,0:T(8,128)(2,1)} %right.1, bf16[2,16,256]{2,1,0:T(8,128)(2,1)} %broadcast_in_dim.19.act, bf16[9,16,16]{2,1,0:T(8,128)(2,1)} %bitcast.4, bf16[9,16,16]{2,1,0:T(8,128)(2,1)} %bitcast.5), custom_call_target="tpu_custom_call" | custom-call | tf_op jit(solution)/shard_map/cost_volume/pallas_call | solution.py:437
  49.7 1.9 %copy.13 = f32[2,256,256]{2,1,0:T(8,128)} copy(f32[2,256,256]{2,1,0:T(8,128)} %cost_volume.1) | data formatting | bytes 1048576
  (4 shorter events, 0.0 us)
Async XLA Ops:
  0.0 0.7 %copy-start.2 = (s32[1,4]{1,0:T(1,128)S(1)}, s32[1,4]{1,0:T(1,128)}, u32[]{:S(2)}) copy-start(s32[1,4]{1,0:T(1,128)} %param.10) | copy-start | bytes 52
  0.7 0.7 %copy-start.1 = (s32[1,4,2]{1,2,0:T(2,128)S(1)}, s32[1,4,2]{1,2,0:T(2,128)}, u32[]{:S(2)}) copy-start(s32[1,4,2]{1,2,0:T(2,128)} %param.9) | copy-start | bytes 100
  1.4 0.7 %copy-start = (bf16[17,16]{0,1:T(8,128)(2,1)S(1)}, bf16[17,16]{0,1:T(8,128)(2,1)}, u32[]{:S(2)}) copy-start(bf16[17,16]{0,1:T(8,128)(2,1)} %param.13) | copy-start | bytes 1636

commit v4 on v3

--- a/solution.py
+++ b/solution.py
@@ -54,7 +54,7 @@
     strip = left.shape[1] - 2 * PAD
     tiles = strip // BLK
     blocks = right.shape[1] // BLK
-    chunk = 32
+    chunk = 64
     chan = lax.broadcasted_iota(jnp.int32, (G, C), 1) // CG
     grp = lax.broadcasted_iota(jnp.int32, (G, C), 0)
     diag = (chan == grp).astype(jnp.float32).astype(jnp.bfloat16)

time: 51.8 us -> 51.8 us (level)
  no operation moved by 1% of the time
where the time goes in v4:
time: 51.8 us; the launch traced here: 51.6 us
  Pallas kernels  46.9 us (91%)
  local copies, waits for them, and re-layouts  4.56 us (9%)
    pallas_call x1, Pallas kernels, body(): pl.pallas_call(kernel, out_shape=jax.ShapeDtypeStruct((rows, strip, ND),...  46.9 us
    unnamed x7, local copies, waits for them, and re-layouts  3.27 us

profile of v4, /device:TPU:17, one launch (start us, length us, event | category | flops | bytes accessed | tf_op | source)
XLA Modules:
  0.0 51.6 jit_solution(7155243656234852723)
XLA Ops:
  0.0 0.0 copy-start.2
  0.0 0.7 %copy-done.2 = s32[1,4]{1,0:T(1,128)S(1)} copy-done((s32[1,4]{1,0:T(1,128)S(1)}, s32[1,4]{1,0:T(1,128)}, u32[]{:S(2)}) %copy-start.2) | copy-done | bytes 40
  0.7 0.0 copy-start.1
  0.7 0.7 %copy-done.1 = s32[1,4,2]{1,2,0:T(2,128)S(1)} copy-done((s32[1,4,2]{1,2,0:T(2,128)S(1)}, s32[1,4,2]{1,2,0:T(2,128)}, u32[]{:S(2)}) %copy-start.1) | copy-done | bytes 56
  1.3 0.1 and_reduce_fusion
  1.4 0.0 copy-start
  1.5 0.6 %broadcast_in_dim.19.act = bf16[2,16,256]{2,1,0:T(8,128)(2,1)} broadcast(bf16[16,256]{1,0:T(8,128)(2,1)S(1)} %pad.4), dimensions={1,2} | broadcast | bytes 24576 | tf_op jit(solution)/shard_map/broadcast_in_dim | solution.py:432
  2.1 0.1 copy-done
  2.1 0.7 %copy.11.dw = f32[17,16]{1,0:T(8,128)} copy(bf16[17,16]{0,1:T(8,128)(2,1)S(1)} %copy-done) | data formatting | bytes 1632 | tf_op jit(solution)/shard_map/convert_element_type | solution.py:467
  2.8 46.9 %cost_volume.1 = f32[2,256,256]{2,1,0:T(8,128)} custom-call(f32[17,16]{1,0:T(8,128)} %copy.11.dw, bf16[2,256,256]{2,1,0:T(8,128)(2,1)} %left.1, bf16[2,256,256]{2,1,0:T(8,128)(2,1)} %right.1, bf16[2,16,256]{2,1,0:T(8,128)(2,1)} %broadcast_in_dim.19.act, bf16[9,16,16]{2,1,0:T(8,128)(2,1)} %bitcast.4, bf16[9,16,16]{2,1,0:T(8,128)(2,1)} %bitcast.5), custom_call_target="tpu_custom_call" | custom-call | tf_op jit(solution)/shard_map/cost_volume/pallas_call | solution.py:437
  49.7 1.9 %copy.13 = f32[2,256,256]{2,1,0:T(8,128)} copy(f32[2,256,256]{2,1,0:T(8,128)} %cost_volume.1) | data formatting | bytes 1048576
  (4 shorter events, 0.0 us)
Async XLA Ops:
  0.0 0.7 %copy-start.2 = (s32[1,4]{1,0:T(1,128)S(1)}, s32[1,4]{1,0:T(1,128)}, u32[]{:S(2)}) copy-start(s32[1,4]{1,0:T(1,128)} %param.10) | copy-start | bytes 52
  0.7 0.7 %copy-start.1 = (s32[1,4,2]{1,2,0:T(2,128)S(1)}, s32[1,4,2]{1,2,0:T(2,128)}, u32[]{:S(2)}) copy-start(s32[1,4,2]{1,2,0:T(2,128)} %param.9) | copy-start | bytes 100
  1.4 0.7 %copy-start = (bf16[17,16]{0,1:T(8,128)(2,1)S(1)}, bf16[17,16]{0,1:T(8,128)(2,1)}, u32[]{:S(2)}) copy-start(bf16[17,16]{0,1:T(8,128)(2,1)} %param.13) | copy-start | bytes 1636
